TPU v7x, 256 devices: a whole 4x4x8 slice. The times are simulated.
256 devices in a mesh: dp: 32 (over z, y), ctx: 8 (over x, core).
Axes of the slice: x: 4, y: 4, z: 8, core: 2. Of those that a mesh axis runs over, the one named last changes fastest.
Arguments:
- query_rows: bfloat16 [32768, 2048], P(('dp', 'ctx')), may hold values from -6 to 6
- key_rows: bfloat16 [32768, 2048], P(('dp', 'ctx')), may hold values from -6 to 6
- value_rows: bfloat16 [32768, 2048], P(('dp', 'ctx')), may hold values from -6 to 6
- target: bfloat16 [32768, 1536], P(('dp', 'ctx')), may hold values from -18 to 18
- w_out: bfloat16 [2048, 1536], replicated, may hold values from -0.125 to 0.125
- clip_lengths: int32 [32, 4], P('dp'), may hold values from 1 to 512, 1024 in all within a row
- timesteps: int32 [32, 4], P('dp'), may hold values from 0 to 999
- tile_pattern: int32 [32, 8, 8], P('dp'), may hold values 0 or 1
- tau_prev: float32 [1], replicated, may hold values from 1 to 4
Outputs:
- query_grad: bfloat16 [32768, 2048], P(('dp', 'ctx'))
- key_grad: bfloat16 [32768, 2048], P(('dp', 'ctx'))
- value_grad: bfloat16 [32768, 2048], P(('dp', 'ctx'))
- weight_grad: float32 [2048, 1536], P('ctx', 'dp')
Inputs may be any that keep to these rules, and one draw needn't show every extreme that they name: `clip_lengths`: each row of clip lengths sums to 1024, and its largest entry is 512.
All inputs are finite; a program needn't handle non-finite values. No bound on the sum of `tile_pattern` on one device may be relied on, other than what follows from the above.
Results may differ from a plain program's by a relative error of at most 0.019.
Values may be sent and summed in bfloat16 or wider, within the bound.
No kernel may reach another device: no remote copies, remote signals or barrier semaphores. Data moves between devices by JAX's collectives and lax.ppermute only.
A program may use at most 128 MiB of HBM per device.

v0:
```python
import math
import jax
import jax.numpy as jnp
from jax import lax
from jax.sharding import Mesh
from jax.sharding import PartitionSpec as P

HD = 128
OUT = 1536
CLIPS = 4
TILE = 128
DP = ("dp_0", "dp_1")
DP_CTX = ("dp_0", "dp_1", "ctx")
MOMENTUM = 0.9


def sent_to_all(array, axis):
    copies = jnp.broadcast_to(array, (lax.axis_size(axis), *array.shape))
    return lax.all_to_all(copies, axis, split_axis=0, concat_axis=0, tiled=True)


def over_copies(array, axis):
    everything = sent_to_all(array, axis)
    return jnp.sum(everything, axis=0)


def summed_rows(array, axes, dim):
    if not axes:
        return array
    nearer = lax.psum_scatter(array, axes[0], scatter_dimension=dim, tiled=True)
    return summed_rows(nearer, axes[1:], dim)


def clip_index(lengths_row, positions):
    ends = jnp.cumsum(lengths_row)
    return jnp.sum((positions[:, None] >= ends[None, :]).astype(jnp.int32), axis=1)


def attention_mask(clip_ids, pattern, row_total):
    tiles = row_total // TILE
    tile_ok = (
        jnp.broadcast_to(pattern[:, None, :, None], (tiles, TILE, tiles, TILE)).reshape(
            row_total, row_total
        )
        > 0
    )
    tile_ids = jnp.arange(row_total, dtype=jnp.int32) // TILE
    same_tile = tile_ids[:, None] == tile_ids[None, :]
    return (clip_ids[:, None] == clip_ids[None, :]) & (tile_ok | same_tile)


def head_probs(query_head, key_head, allowed):
    score_scale = 1.0 / math.sqrt(HD)
    scores = (
        lax.dot_general(
            query_head, key_head, (((1,), (1,)), ((), ())), preferred_element_type=jnp.float32
        )
        * score_scale
    )
    scores = jnp.where(allowed, scores, -1e30)
    row_max = jnp.max(scores, axis=1)
    unnorm = jnp.where(allowed, jnp.exp(scores - row_max[:, None]), 0.0)
    row_total = jnp.sum(unnorm, axis=1)
    return unnorm / row_total[:, None]


def head_backward(query_head, key_head, value_head, out_head, grad_head, allowed):
    score_scale = 1.0 / math.sqrt(HD)
    probs = head_probs(query_head, key_head, allowed)
    probs_low = probs.astype(jnp.bfloat16)
    value_grad = lax.dot_general(
        probs_low, grad_head, (((0,), (0,)), ((), ())), preferred_element_type=jnp.float32
    ).astype(jnp.bfloat16)
    prob_grad = lax.dot_general(
        grad_head, value_head, (((1,), (1,)), ((), ())), preferred_element_type=jnp.float32
    )
    delta = jnp.sum(grad_head.astype(jnp.float32) * out_head.astype(jnp.float32), axis=1)
    score_grad = (probs * (prob_grad - delta[:, None])).astype(jnp.bfloat16)
    query_grad = (
        jnp.dot(score_grad, key_head, preferred_element_type=jnp.float32) * score_scale
    ).astype(jnp.bfloat16)
    key_grad = (
        lax.dot_general(
            score_grad, query_head, (((0,), (0,)), ((), ())), preferred_element_type=jnp.float32
        )
        * score_scale
    ).astype(jnp.bfloat16)
    return (query_grad, key_grad, value_grad)


def superloss_weight(clip_loss, tau_now):
    argument = jnp.maximum(-0.3, 0.5 * (clip_loss - tau_now))
    branch = jnp.log1p(argument)
    for sweep in range(5):
        exp_value = jnp.exp(branch)
        branch = branch - (branch * exp_value - argument) / (exp_value * (branch + 1.0))
    return jnp.exp(-branch)


def on_device(
    query_rows, key_rows, value_rows, target, w_out, clip_lengths, timesteps, tile_pattern, tau_prev
):
    row_count = query_rows.shape[0]
    ctx_count = lax.axis_size("ctx")
    dp_count = lax.axis_size(DP)
    pack_rows = row_count * ctx_count
    ctx_place = lax.axis_index("ctx")
    query_head, key_head, value_head = (
        lax.all_to_all(query_rows, "ctx", split_axis=1, concat_axis=0, tiled=True),
        lax.all_to_all(key_rows, "ctx", split_axis=1, concat_axis=0, tiled=True),
        lax.all_to_all(value_rows, "ctx", split_axis=1, concat_axis=0, tiled=True),
    )
    lengths_row = clip_lengths[0]
    clip_pack = clip_index(lengths_row, jnp.arange(pack_rows, dtype=jnp.int32))
    allowed = attention_mask(clip_pack, tile_pattern[0], pack_rows)
    width_dev = query_head.shape[1]
    heads_dev = width_dev // HD
    head_outs = []
    for head in range(heads_dev):
        cols = slice(head * HD, (head + 1) * HD)
        probs = head_probs(query_head[:, cols], key_head[:, cols], allowed)
        head_outs.append(
            jnp.dot(
                probs.astype(jnp.bfloat16), value_head[:, cols], preferred_element_type=jnp.float32
            ).astype(jnp.bfloat16)
        )
    out_head = jnp.concatenate(head_outs, axis=1)
    out_rows = lax.all_to_all(out_head, "ctx", split_axis=0, concat_axis=1, tiled=True)
    predicted = jnp.dot(out_rows, w_out, preferred_element_type=jnp.float32)
    residue = predicted - target.astype(jnp.float32)
    row_squares = jnp.sum(residue * residue, axis=1)
    positions = ctx_place * row_count + jnp.arange(row_count, dtype=jnp.int32)
    clip_rows = clip_index(lengths_row, positions)
    onehot = (clip_rows[:, None] == jnp.arange(CLIPS, dtype=jnp.int32)[None, :]).astype(jnp.float32)
    partial_value = jnp.sum(row_squares[:, None] * onehot, axis=0)
    clip_len = lengths_row.astype(jnp.float32)
    step_weight = 1.0 + timesteps[0].astype(jnp.float32) / 250.0
    clip_sq = over_copies(partial_value, "ctx")
    clip_loss = step_weight * clip_sq / (clip_len * OUT)
    loss_sum = over_copies(jnp.sum(clip_loss), DP)
    loss_mean = loss_sum / (dp_count * CLIPS)
    tau_now = MOMENTUM * tau_prev[0] + (1.0 - MOMENTUM) * loss_mean
    confidence = superloss_weight(clip_loss, tau_now)
    tokens_all = pack_rows * dp_count
    clip_scale = confidence * step_weight
    row_scale = jnp.sum(onehot * clip_scale[None, :], axis=1)
    pred_grad = (residue * row_scale[:, None]).astype(jnp.bfloat16)
    norm_factor = 1.0 / math.sqrt(tokens_all)
    pred_pack = lax.all_gather(pred_grad, "ctx", axis=0, tiled=True)
    w_block = lax.dynamic_slice_in_dim(w_out, ctx_place * width_dev, width_dev, 0)
    grad_head = lax.dot_general(
        pred_pack, w_block, (((1,), (1,)), ((), ())), preferred_element_type=jnp.float32
    ).astype(jnp.bfloat16)
    block_terms = (
        lax.dot_general(
            out_head, pred_pack, (((0,), (0,)), ((), ())), preferred_element_type=jnp.float32
        )
        * norm_factor
    )
    weight_grad = summed_rows(block_terms.astype(jnp.bfloat16), DP, 1).astype(jnp.float32)
    parts_q, parts_k, parts_v = ([], [], [])
    for head in range(heads_dev):
        cols = slice(head * HD, (head + 1) * HD)
        grads = head_backward(
            query_head[:, cols],
            key_head[:, cols],
            value_head[:, cols],
            out_head[:, cols],
            grad_head[:, cols],
            allowed,
        )
        parts_q.append(grads[0])
        parts_k.append(grads[1])
        parts_v.append(grads[2])
    query_back, key_back, value_back = (
        lax.all_to_all(
            jnp.concatenate(parts_q, axis=1), "ctx", split_axis=0, concat_axis=1, tiled=True
        ),
        lax.all_to_all(
            jnp.concatenate(parts_k, axis=1), "ctx", split_axis=0, concat_axis=1, tiled=True
        ),
        lax.all_to_all(
            jnp.concatenate(parts_v, axis=1), "ctx", split_axis=0, concat_axis=1, tiled=True
        ),
    )
    return (query_back, key_back, value_back, weight_grad)


def solution(mesh):
    finer = Mesh(mesh.devices.reshape(8, 4, mesh.shape["ctx"]), ("dp_0", "dp_1", "ctx"))
    return jax.shard_map(
        on_device,
        mesh=finer,
        in_specs=(
            P(DP_CTX, None),
            P(DP_CTX, None),
            P(DP_CTX, None),
            P(DP_CTX, None),
            P(),
            P(DP, None),
            P(DP, None),
            P(DP, None, None),
            P(),
        ),
        out_specs=(P(DP_CTX, None), P(DP_CTX, None), P(DP_CTX, None), P("ctx", DP)),
        check_vma=False,
    )
```

profile of v0, /device:TPU:4, one launch (start us, length us, event | category | flops | bytes accessed | tf_op | source)
XLA Modules:
  0.0 216.0 jit_solution(11657505855100650030)
XLA Ops:
  7.2 2.1 copy.72
  9.3 5.6 %all-to-all-start = ((bf16[128,8,256]{0,2,1:T(8,128)(2,1)}), bf16[128,8,256]{0,2,1:T(8,128)(2,1)S(1)}, u32[]{:S(2)}, u32[]{:S(2)}) async-start(bf16[128,8,256]{0,2,1:T(8,128)(2,1)} %bitcast.3), calls=%async_computation | async-start | bytes 1048576 | tf_op jit(solution)/shard_map/all_to_all | solution.py:109
  14.9 2.0 copy.74
  17.0 5.1 %all-to-all-done = bf16[128,8,256]{0,2,1:T(8,128)(2,1)S(1)} async-done(((bf16[128,8,256]{0,2,1:T(8,128)(2,1)}), bf16[128,8,256]{0,2,1:T(8,128)(2,1)S(1)}, u32[]{:S(2)}, u32[]{:S(2)}) %all-to-all-start) | async-done | bytes 524320 | tf_op jit(solution)/shard_map/all_to_all | solution.py:109
  22.1 6.6 %all-to-all-start.1 = ((bf16[128,8,256]{0,2,1:T(8,128)(2,1)}), bf16[128,8,256]{0,2,1:T(8,128)(2,1)S(1)}, u32[]{:S(2)}, u32[]{:S(2)}) async-start(bf16[128,8,256]{0,2,1:T(8,128)(2,1)} %bitcast.6), calls=%async_computation.1 | async-start | bytes 1048576 | tf_op jit(solution)/shard_map/all_to_all | solution.py:110
  28.7 1.0 copy.76
  29.7 6.2 %all-to-all-done.1 = bf16[128,8,256]{0,2,1:T(8,128)(2,1)S(1)} async-done(((bf16[128,8,256]{0,2,1:T(8,128)(2,1)}), bf16[128,8,256]{0,2,1:T(8,128)(2,1)S(1)}, u32[]{:S(2)}, u32[]{:S(2)}) %all-to-all-start.1) | async-done | bytes 524320 | tf_op jit(solution)/shard_map/all_to_all | solution.py:110
  35.8 6.6 %all-to-all-start.2 = ((bf16[128,8,256]{0,2,1:T(8,128)(2,1)}), bf16[128,8,256]{0,2,1:T(8,128)(2,1)S(1)}, u32[]{:S(2)}, u32[]{:S(2)}) async-start(bf16[128,8,256]{0,2,1:T(8,128)(2,1)} %bitcast.9), calls=%async_computation.2 | async-start | bytes 1048576 | tf_op jit(solution)/shard_map/all_to_all | solution.py:111
  43.2 6.3 %all-to-all-done.2 = bf16[128,8,256]{0,2,1:T(8,128)(2,1)S(1)} async-done(((bf16[128,8,256]{0,2,1:T(8,128)(2,1)}), bf16[128,8,256]{0,2,1:T(8,128)(2,1)S(1)}, u32[]{:S(2)}, u32[]{:S(2)}) %all-to-all-start.2) | async-done | bytes 524320 | tf_op jit(solution)/shard_map/all_to_all | solution.py:111
  49.8 0.7 fusion.21
  50.9 2.5 %fusion.1 = (f32[1024]{0:T(1024)S(1)}, f32[1024]{0:T(1024)S(1)}, pred[1024,1024]{0,1:T(32,128)(4,1)S(1)}, f32[1024,1024]{0,1:T(8,128)S(1)}) fusion(f32[1024,1024]{0,1:T(8,128)S(1)} %fusion.21, s32[1024]{0:T(1024)S(1)} %add_select_fusion, pred[128,8,8,128]{3,2,1,0:T(8,128)(4,1)S(1)} %bitcast.96, s32[1024]{0:T(1024)S(1)} %convert_reduce_fusion, ...), kind=kOutput, calls=%fused_computation.8 | convolution fusion | flops 278919168 | bytes 11034624 | tf_op jit(solution)/shard_map/dot_general | solution.py:55
  53.4 2.2 %fusion.5 = (f32[1024]{0:T(1024)S(1)}, f32[1024]{0:T(1024)S(1)}) fusion(pred[1024,1024]{0,1:T(32,128)(4,1)S(1)} %get-tuple-element.22, f32[1024,1024]{0,1:T(8,128)S(1)} %get-tuple-element.23, f32[1024]{0:T(1024)S(1)} %get-tuple-element.18, f32[1024]{0:T(1024)S(1)} %get-tuple-element.19, f32[1024,1024]{0,1:T(8,128)S(1)} %fusion.21), kind=kLoop, calls=%fused_computation.14 | loop fusion | flops 10483712 | bytes 9453568 | tf_op jit(solution)/shard_map/reduce_sum | solution.py:63
  55.6 1.5 convolution_convert_fusion.3
  57.2 1.5 convolution_convert_fusion.4
  58.8 0.9 copy_bitcast_fusion.3
  59.6 6.6 %all-to-all-start.3 = ((bf16[8,128,256]{1,2,0:T(8,128)(2,1)}), bf16[8,128,256]{1,2,0:T(8,128)(2,1)S(1)}, u32[]{:S(2)}, u32[]{:S(2)}) async-start(bf16[8,128,256]{1,2,0:T(8,128)(2,1)} %copy_bitcast_fusion.3), calls=%async_computation.3 | async-start | bytes 1048576 | tf_op jit(solution)/shard_map/all_to_all | solution.py:128
  66.3 7.1 %all-to-all-done.3 = bf16[8,128,256]{1,2,0:T(8,128)(2,1)S(1)} async-done(((bf16[8,128,256]{1,2,0:T(8,128)(2,1)}), bf16[8,128,256]{1,2,0:T(8,128)(2,1)S(1)}, u32[]{:S(2)}, u32[]{:S(2)}) %all-to-all-start.3) | async-done | bytes 524320 | tf_op jit(solution)/shard_map/all_to_all | solution.py:128
  73.4 3.9 %multiply_reduce_fusion = (f32[128]{0:T(128)S(1)}, f32[128,1536]{1,0:T(8,128)S(1)}) fusion(bf16[128,1536]{1,0:T(8,128)(2,1)} %param.12, bf16[128,2048]{0,1:T(8,128)(2,1)S(1)} %bitcast.85, bf16[2048,1536]{1,0:T(8,128)(2,1)} %param.13), kind=kOutput, calls=%fused_computation.36 | convolution fusion | flops 806092672 | bytes 7995904 | tf_op jit(solution)/shard_map/dot_general | solution.py:129
  77.4 8.4 %all_to_all.145 = f32[8,1,4]{2,1,0:T(1,128)S(1)} all-to-all(f32[8,1,4]{2,1,0:T(1,128)S(1)} %broadcast_in_dim.22), channel_id=1, replica_groups=mesh['dp_0'=8,'dp_1'=4,'ctx'=8] {'ctx'}, dimensions={0} | all-to-all | bytes 256 | tf_op jit(solution)/shard_map/all_to_all | solution.py:19
  86.5 1.3 broadcast_in_dim.23
  87.8 10.7 %all-to-all-start.5 = ((f32[32,1,1]{2,1,0:T(1,128)}), f32[32,1,1]{2,1,0:T(1,128)S(1)}, u32[]{:S(2)}, u32[]{:S(2)}) async-start(f32[32,1,1]{2,1,0:T(1,128)} %broadcast_in_dim.23), calls=%async_computation.5 | async-start | bytes 32768 | tf_op jit(solution)/shard_map/all_to_all | solution.py:19
  99.1 9.0 %all-to-all-done.5 = f32[32,1,1]{2,1,0:T(1,128)S(1)} async-done(((f32[32,1,1]{2,1,0:T(1,128)}), f32[32,1,1]{2,1,0:T(1,128)S(1)}, u32[]{:S(2)}, u32[]{:S(2)}) %all-to-all-start.5) | async-done | bytes 160 | tf_op jit(solution)/shard_map/all_to_all | solution.py:19
  108.1 0.6 reduce_sum.127
  109.6 0.9 multiply_convert_fusion.2
  110.7 23.2 %all-gather.2.cloned.1.call-done = bf16[1024,1536]{1,0:T(8,128)(2,1)} async-done(((bf16[128,1536]{1,0:T(8,128)(2,1)}), bf16[1024,1536]{1,0:T(8,128)(2,1)}) %all-gather.2.cloned.1.call-update) | async-done | bytes 3145744 | tf_op jit(solution)/shard_map/all_gather | solution.py:149
  133.9 3.2 %convolution_convert_fusion = bf16[1024,256]{0,1:T(8,128)(2,1)S(1)} fusion(bf16[1024,1536]{1,0:T(8,128)(2,1)} %all-gather.2.cloned.1.call-done, bf16[2048,1536]{1,0:T(8,128)(2,1)} %param.13, s32[]{:T(128)S(6)} %select_n.38), kind=kOutput, calls=%fused_computation.17 | convolution fusion | flops 805568512 | bytes 4456452 | tf_op jit(solution)/shard_map/dot_general | solution.py:151
  137.3 1.5 convolution_convert_fusion.2
  138.9 0.8 copy-done.1
  139.7 1.5 convolution_convert_fusion.1
  141.6 2.3 %fusion.3 = bf16[256,1536]{0,1:T(8,128)(2,1)} fusion(bf16[1024,1536]{1,0:T(8,128)(2,1)S(1)} %copy-done.19, bf16[1024,128]{0,1:T(8,128)(2,1)S(1)} %convolution_convert_fusion.3, bf16[1024,128]{0,1:T(8,128)(2,1)S(1)} %convolution_convert_fusion.4), kind=kOutput, calls=%fused_computation.11 | convolution fusion | flops 807141376 | bytes 4456448 | tf_op jit(solution)/shard_map/dot_general | solution.py:155
  143.9 0.9 copy_bitcast_fusion
  144.8 5.3 %all-to-all-start.8 = ((bf16[8,128,256]{1,2,0:T(8,128)(2,1)}), bf16[8,128,256]{1,2,0:T(8,128)(2,1)S(1)}, u32[]{:S(2)}, u32[]{:S(2)}) async-start(bf16[8,128,256]{1,2,0:T(8,128)(2,1)} %copy_bitcast_fusion), calls=%async_computation.8 | async-start | bytes 1048576 | tf_op jit(solution)/shard_map/all_to_all | solution.py:182
  150.2 5.1 %multiply_convert_fusion.1 = bf16[1024,1024]{0,1:T(8,128)(2,1)S(1)} fusion(f32[1024]{0:T(1024)S(1)} %get-tuple-element.20, bf16[1024,256]{1,0:T(8,128)(2,1)} %bitcast.99, bf16[1024,256]{0,1:T(8,128)(2,1)} %copy-done.14, f32[1024]{0:T(1024)S(1)} %get-tuple-element.16, pred[1024,1024]{0,1:T(32,128)(4,1)} %copy-done.9, f32[1024]{0:T(1024)S(1)} %get-tuple-element.18, ...), kind=kOutput, calls=%fused_computation.1 | convolution fusion | flops 276824064 | bytes 7876608 | tf_op jit(solution)/shard_map/dot_general | solution.py:74
  155.3 1.7 multiply_convert_fusion
  157.1 0.8 fusion.10
  157.9 0.8 fusion.11
  158.8 0.9 copy_bitcast_fusion.1
  159.7 4.8 %all-to-all-start.7 = ((bf16[8,128,256]{1,2,0:T(8,128)(2,1)}), bf16[8,128,256]{1,2,0:T(8,128)(2,1)S(1)}, u32[]{:S(2)}, u32[]{:S(2)}) async-start(bf16[8,128,256]{1,2,0:T(8,128)(2,1)} %copy_bitcast_fusion.1), calls=%async_computation.7 | async-start | bytes 1048576 | tf_op jit(solution)/shard_map/all_to_all | solution.py:179
  164.5 1.6 fusion.8
  166.7 0.9 copy_bitcast_fusion.2
  167.6 4.0 %all-to-all-done.7 = bf16[8,128,256]{1,2,0:T(8,128)(2,1)S(1)} async-done(((bf16[8,128,256]{1,2,0:T(8,128)(2,1)}), bf16[8,128,256]{1,2,0:T(8,128)(2,1)S(1)}, u32[]{:S(2)}, u32[]{:S(2)}) %all-to-all-start.7) | async-done | bytes 524320 | tf_op jit(solution)/shard_map/all_to_all | solution.py:179
  171.6 6.6 %all-to-all-start.6 = ((bf16[8,128,256]{1,2,0:T(8,128)(2,1)}), bf16[8,128,256]{1,2,0:T(8,128)(2,1)S(1)}, u32[]{:S(2)}, u32[]{:S(2)}) async-start(bf16[8,128,256]{1,2,0:T(8,128)(2,1)} %copy_bitcast_fusion.2), calls=%async_computation.6 | async-start | bytes 1048576 | tf_op jit(solution)/shard_map/all_to_all | solution.py:176
  178.2 5.6 %reduce-scatter.3.cloned.1.call-done = bf16[256,192]{0,1:T(8,128)(2,1)} async-done(((bf16[256,1536]{0,1:T(8,128)(2,1)}), bf16[256,192]{0,1:T(8,128)(2,1)}) %reduce-scatter.3.cloned.1.call-update) | async-done | bytes 98320 | tf_op jit(solution)/shard_map/reduce_scatter | solution.py:30
  183.8 1.0 copy.88
  184.8 1.0 copy.87
  185.8 1.0 copy.86
  186.8 21.3 %reduce-scatter.5.cloned.1.call-done = bf16[256,48]{0,1:T(8,128)(2,1)} async-done(((bf16[256,192]{0,1:T(8,128)(2,1)}), bf16[256,48]{0,1:T(8,128)(2,1)}) %reduce-scatter.5.cloned.1.call-update) | async-done | bytes 24592 | tf_op jit(solution)/shard_map/reduce_scatter | solution.py:30
  208.1 1.4 convert_element_type.106
  (66 shorter events, 3.8 us)
Async XLA Ops:
  7.2 21.5 %copy-start.11 = (bf16[128,2048]{1,0:T(8,128)(2,1)S(1)}, bf16[128,2048]{1,0:T(8,128)(2,1)}, u32[]{:S(2)}) copy-start(bf16[128,2048]{1,0:T(8,128)(2,1)} %param.11) | copy-start | bytes 1572868
  7.2 35.2 %copy-start.16 = (s32[1,8,8]{2,1,0:T(8,128)S(1)}, s32[1,8,8]{2,1,0:T(8,128)}, u32[]{:S(2)}) copy-start(s32[1,8,8]{2,1,0:T(8,128)} %param.16) | copy-start | bytes 772
  7.2 35.3 %copy-start.17 = (s32[1,4]{1,0:T(1,128)S(1)}, s32[1,4]{1,0:T(1,128)}, u32[]{:S(2)}) copy-start(s32[1,4]{1,0:T(1,128)} %param.14) | copy-start | bytes 52
  9.3 12.8 %all-to-all-start = ((bf16[128,8,256]{0,2,1:T(8,128)(2,1)}), bf16[128,8,256]{0,2,1:T(8,128)(2,1)S(1)}, u32[]{:S(2)}, u32[]{:S(2)}) async-start(bf16[128,8,256]{0,2,1:T(8,128)(2,1)} %bitcast.3), calls=%async_computation | async-start | bytes 1048576 | tf_op jit(solution)/shard_map/all_to_all | solution.py:109
  22.1 13.7 %all-to-all-start.1 = ((bf16[128,8,256]{0,2,1:T(8,128)(2,1)}), bf16[128,8,256]{0,2,1:T(8,128)(2,1)S(1)}, u32[]{:S(2)}, u32[]{:S(2)}) async-start(bf16[128,8,256]{0,2,1:T(8,128)(2,1)} %bitcast.6), calls=%async_computation.1 | async-start | bytes 1048576 | tf_op jit(solution)/shard_map/all_to_all | solution.py:110
  35.8 13.7 %all-to-all-start.2 = ((bf16[128,8,256]{0,2,1:T(8,128)(2,1)}), bf16[128,8,256]{0,2,1:T(8,128)(2,1)S(1)}, u32[]{:S(2)}, u32[]{:S(2)}) async-start(bf16[128,8,256]{0,2,1:T(8,128)(2,1)} %bitcast.9), calls=%async_computation.2 | async-start | bytes 1048576 | tf_op jit(solution)/shard_map/all_to_all | solution.py:111
  43.2 10.1 %copy-start.7 = (bf16[8,128,256]{2,1,0:T(8,128)(2,1)}, bf16[8,128,256]{2,1,0:T(8,128)(2,1)S(1)}, u32[]{:S(2)}) copy-start(bf16[8,128,256]{2,1,0:T(8,128)(2,1)S(1)} %copy.75) | copy-start | bytes 1572868
  49.8 7.4 %copy-start.12 = (bf16[8,128,256]{2,1,0:T(8,128)(2,1)}, bf16[8,128,256]{2,1,0:T(8,128)(2,1)S(1)}, u32[]{:S(2)}) copy-start(bf16[8,128,256]{2,1,0:T(8,128)(2,1)S(1)} %copy.77) | copy-start | bytes 1572868
  50.5 5.1 %copy-start = (f32[1024,1024]{0,1:T(8,128)}, f32[1024,1024]{0,1:T(8,128)S(1)}, u32[]{:S(2)}) copy-start(f32[1024,1024]{0,1:T(8,128)S(1)} %fusion.21) | copy-start | bytes 12582916
  53.4 3.8 %copy-start.3 = (f32[1024,1024]{0,1:T(8,128)}, f32[1024,1024]{0,1:T(8,128)S(1)}, u32[]{:S(2)}) copy-start(f32[1024,1024]{0,1:T(8,128)S(1)} %get-tuple-element.23) | copy-start | bytes 12582916
  53.4 85.5 %copy-start.9 = (pred[1024,1024]{0,1:T(32,128)(4,1)}, pred[1024,1024]{0,1:T(32,128)(4,1)S(1)}, u32[]{:S(2)}) copy-start(pred[1024,1024]{0,1:T(32,128)(4,1)S(1)} %get-tuple-element.22) | copy-start | bytes 3145732
  59.6 13.7 %all-to-all-start.3 = ((bf16[8,128,256]{1,2,0:T(8,128)(2,1)}), bf16[8,128,256]{1,2,0:T(8,128)(2,1)S(1)}, u32[]{:S(2)}, u32[]{:S(2)}) async-start(bf16[8,128,256]{1,2,0:T(8,128)(2,1)} %copy_bitcast_fusion.3), calls=%async_computation.3 | async-start | bytes 1048576 | tf_op jit(solution)/shard_map/all_to_all | solution.py:128
  66.2 19.7 %copy-start.18 = (s32[1,4]{1,0:T(1,128)S(1)}, s32[1,4]{1,0:T(1,128)}, u32[]{:S(2)}) copy-start(s32[1,4]{1,0:T(1,128)} %param.15) | copy-start | bytes 52
  87.8 20.3 %all-to-all-start.5 = ((f32[32,1,1]{2,1,0:T(1,128)}), f32[32,1,1]{2,1,0:T(1,128)S(1)}, u32[]{:S(2)}, u32[]{:S(2)}) async-start(f32[32,1,1]{2,1,0:T(1,128)} %broadcast_in_dim.23), calls=%async_computation.5 | async-start | bytes 32768 | tf_op jit(solution)/shard_map/all_to_all | solution.py:19
  98.4 35.5 %all-gather.2.cloned.1.call-start = ((), (), s32[]{:S(2)}) async-start(), calls=%async_computation.11 | async-start | bytes 3538944 | tf_op jit(solution)/shard_map/all_gather | solution.py:149
  110.5 73.3 %reduce-scatter.3.cloned.1.call-start = ((), (), s32[]{:S(2)}) async-start(), calls=%async_computation.12 | async-start | bytes 884736 | tf_op jit(solution)/shard_map/reduce_scatter | solution.py:30
  133.9 3.4 %copy-start.4 = (f32[1024,1024]{0,1:T(8,128)S(1)}, f32[1024,1024]{0,1:T(8,128)}, u32[]{:S(2)}) copy-start(f32[1024,1024]{0,1:T(8,128)} %copy-done.3) | copy-start | bytes 12582916
  137.3 3.9 %copy-start.14 = (bf16[1024,256]{0,1:T(8,128)(2,1)}, bf16[1024,256]{0,1:T(8,128)(2,1)S(1)}, u32[]{:S(2)}) copy-start(bf16[1024,256]{0,1:T(8,128)(2,1)S(1)} %convolution_convert_fusion) | copy-start | bytes 1572868
  137.3 2.4 %copy-start.1 = (f32[1024,1024]{0,1:T(8,128)S(1)}, f32[1024,1024]{0,1:T(8,128)}, u32[]{:S(2)}) copy-start(f32[1024,1024]{0,1:T(8,128)} %copy-done) | copy-start | bytes 12582916
  139.7 1.9 copy-start.19
  144.8 14.8 %all-to-all-start.8 = ((bf16[8,128,256]{1,2,0:T(8,128)(2,1)}), bf16[8,128,256]{1,2,0:T(8,128)(2,1)S(1)}, u32[]{:S(2)}, u32[]{:S(2)}) async-start(bf16[8,128,256]{1,2,0:T(8,128)(2,1)} %copy_bitcast_fusion), calls=%async_computation.8 | async-start | bytes 1048576 | tf_op jit(solution)/shard_map/all_to_all | solution.py:182
  150.2 5.1 %copy-start.2 = (f32[1024,1024]{0,1:T(8,128)S(1)}, f32[1024,1024]{0,1:T(8,128)}, u32[]{:S(2)}) copy-start(f32[1024,1024]{0,1:T(8,128)} %copy-done) | copy-start | bytes 12582916
  150.2 5.1 %copy-start.10 = (pred[1024,1024]{0,1:T(32,128)(4,1)S(1)}, pred[1024,1024]{0,1:T(32,128)(4,1)}, u32[]{:S(2)}) copy-start(pred[1024,1024]{0,1:T(32,128)(4,1)} %copy-done.9) | copy-start | bytes 3145732
  150.2 5.2 %copy-start.13 = (bf16[8,128,256]{2,1,0:T(8,128)(2,1)S(1)}, bf16[8,128,256]{2,1,0:T(8,128)(2,1)}, u32[]{:S(2)}) copy-start(bf16[8,128,256]{2,1,0:T(8,128)(2,1)} %copy-done.12) | copy-start | bytes 1572868
  150.2 5.2 %copy-start.15 = (bf16[1024,256]{0,1:T(8,128)(2,1)S(1)}, bf16[1024,256]{0,1:T(8,128)(2,1)}, u32[]{:S(2)}) copy-start(bf16[1024,256]{0,1:T(8,128)(2,1)} %copy-done.14) | copy-start | bytes 1572868
  157.1 1.7 copy-start.5
  159.7 12.0 %all-to-all-start.7 = ((bf16[8,128,256]{1,2,0:T(8,128)(2,1)}), bf16[8,128,256]{1,2,0:T(8,128)(2,1)S(1)}, u32[]{:S(2)}, u32[]{:S(2)}) async-start(bf16[8,128,256]{1,2,0:T(8,128)(2,1)} %copy_bitcast_fusion.1), calls=%async_computation.7 | async-start | bytes 1048576 | tf_op jit(solution)/shard_map/all_to_all | solution.py:179
  164.5 1.7 copy-start.6
  164.5 1.8 copy-start.8
  171.6 14.2 %all-to-all-start.6 = ((bf16[8,128,256]{1,2,0:T(8,128)(2,1)}), bf16[8,128,256]{1,2,0:T(8,128)(2,1)S(1)}, u32[]{:S(2)}, u32[]{:S(2)}) async-start(bf16[8,128,256]{1,2,0:T(8,128)(2,1)} %copy_bitcast_fusion.2), calls=%async_computation.6 | async-start | bytes 1048576 | tf_op jit(solution)/shard_map/all_to_all | solution.py:176
  178.2 29.9 %reduce-scatter.5.cloned.1.call-start = ((), (), s32[]{:S(2)}) async-start(), calls=%async_computation.13 | async-start | bytes 122880 | tf_op jit(solution)/shard_map/reduce_scatter | solution.py:30
Sparse Core Ops, SparseCore 0:
  110.6 23.2 all-gather.1
  144.0 39.6 reduce-scatter.2
  186.3 21.8 reduce-scatter.4
where the time goes:
time: 217 us; the launch traced here: 216 us
  waiting for transfers between devices  87.8 us (40%)
  starting transfers between devices  53 us (24%)
  matrix products  29.4 us (14%)
  between operations  15.4 us (7%)
  local copies, waits for them, and re-layouts  11.8 us (5%)
  other arithmetic  10.1 us (5%)
  blocking collectives  8.45 us (4%)
    reduce_scatter x2, waiting for transfers between devices, summed_rows(): nearer = lax.psum_scatter(array, axes[0], scatter_dimension=dim, tiled=True)  26.9 us
    all_gather x1, waiting for transfers between devices, on_device(): pred_pack = lax.all_gather(pred_grad, 'ctx', axis=0, tiled=True)  23.2 us
    all_to_all x1, starting transfers between devices, sent_to_all(): return lax.all_to_all(copies, axis, split_axis=0, concat_axis=0, tiled=True)  10.7 us
    unnamed x46, local copies, waits for them, and re-layouts  9.48 us
    all_to_all x1, waiting for transfers between devices, sent_to_all(): return lax.all_to_all(copies, axis, split_axis=0, concat_axis=0, tiled=True)  8.99 us
    all_to_all x1, blocking collectives, sent_to_all(): return lax.all_to_all(copies, axis, split_axis=0, concat_axis=0, tiled=True)  8.45 us
    all_to_all x1, waiting for transfers between devices, on_device(): lax.all_to_all(out_head, 'ctx', split_axis=0, concat_axis=1, tiled=True)  7.07 us
    dot_general x2, matrix products, head_backward(): lax.dot_general(grad_head, value_head, (((1,), (1,)), ((), ())), preferre...  6.82 us
  transfers between devices with their start and end apart: 11, of which 9 were waited for; matrix products, arithmetic and copies ran while one was open for 9% of the time, Pallas kernels for 0%

commit v1 on v0

--- a/solution.py
+++ b/solution.py
@@ -146,7 +146,10 @@
     row_scale = jnp.sum(onehot * clip_scale[None, :], axis=1)
     pred_grad = (residue * row_scale[:, None]).astype(jnp.bfloat16)
     norm_factor = 1.0 / math.sqrt(tokens_all)
-    pred_pack = lax.all_gather(pred_grad, "ctx", axis=0, tiled=True)
+    count = lax.axis_size("ctx")
+    pieces = jnp.stack([pred_grad for _ in range(count)])
+    pieces = lax.all_to_all(pieces, "ctx", split_axis=0, concat_axis=0)
+    pred_pack = jnp.concatenate(pieces, axis=0)
     w_block = lax.dynamic_slice_in_dim(w_out, ctx_place * width_dev, width_dev, 0)
     grad_head = lax.dot_general(
         pred_pack, w_block, (((1,), (1,)), ((), ())), preferred_element_type=jnp.float32

time: 217 us -> 239 us (1.10)
  starting transfers between devices: 53 us -> 62.7 us
  waiting for transfers between devices: 87.8 us -> 93.9 us
  matrix products: 29.4 us -> 34.8 us
    all_to_all x0 -> x1, waiting for transfers between devices: none -> 35.4 us  [on_device(): pieces = lax.all_to_all(pieces, 'ctx', split_axis=0, concat_axis=0)]
    all_gather x1 -> x0, waiting for transfers between devices: 23.2 us -> none  [on_device(): pred_pack = lax.all_gather(pred_grad, 'ctx', axis=0, tiled=True)]
    reduce_scatter x2, waiting for transfers between devices: 26.9 us -> 12.8 us  [summed_rows(): nearer = lax.psum_scatter(array, axes[0], scatter_dimension=dim, tiled=True)]
    all_to_all x0 -> x1, starting transfers between devices: none -> 6.75 us  [on_device(): pieces = lax.all_to_all(pieces, 'ctx', split_axis=0, concat_axis=0)]
    all_to_all x1, waiting for transfers between devices: 0.01 us -> 4.41 us  [on_device(): lax.all_to_all(jnp.concatenate(parts_q, axis=1), 'ctx', split_axis=0, con...]
    all_to_all x1, waiting for transfers between devices: 0.01 us -> 3.02 us  [on_device(): lax.all_to_all(jnp.concatenate(parts_v, axis=1), 'ctx', split_axis=0, con...]
    unnamed x46 -> x44, local copies, waits for them, and re-layouts: 9.48 us -> 8.99 us
  transfers between devices with their start and end apart: 11 -> 11, of which waited for: 9 -> 10; matrix products, arithmetic and copies ran while one was open for 9% -> 10% of each run, Pallas kernels for 0% -> 0%
where the time goes in v1:
time: 239 us; the launch traced here: 238 us
  waiting for transfers between devices  93.9 us (39%)
  starting transfers between devices  62.7 us (26%)
  matrix products  34.8 us (15%)
  between operations  15.7 us (7%)
  local copies, waits for them, and re-layouts  13.3 us (6%)
  other arithmetic  9.37 us (4%)
  blocking collectives  8.45 us (4%)
    all_to_all x1, waiting for transfers between devices, on_device(): pieces = lax.all_to_all(pieces, 'ctx', split_axis=0, concat_axis=0)  35.4 us
    reduce_scatter x2, waiting for transfers between devices, summed_rows(): nearer = lax.psum_scatter(array, axes[0], scatter_dimension=dim, tiled=True)  12.8 us
    all_to_all x1, starting transfers between devices, sent_to_all(): return lax.all_to_all(copies, axis, split_axis=0, concat_axis=0, tiled=True)  10.8 us
    unnamed x44, local copies, waits for them, and re-layouts  8.99 us
    all_to_all x1, waiting for transfers between devices, sent_to_all(): return lax.all_to_all(copies, axis, split_axis=0, concat_axis=0, tiled=True)  8.86 us
    all_to_all x1, blocking collectives, sent_to_all(): return lax.all_to_all(copies, axis, split_axis=0, concat_axis=0, tiled=True)  8.45 us
    dot_general x2, matrix products, head_backward(): lax.dot_general(grad_head, value_head, (((1,), (1,)), ((), ())), preferre...  8.12 us
    all_to_all x1, waiting for transfers between devices, on_device(): lax.all_to_all(out_head, 'ctx', split_axis=0, concat_axis=1, tiled=True)  7.07 us
  transfers between devices with their start and end apart: 11, of which 10 were waited for; matrix products, arithmetic and copies ran while one was open for 10% of the time, Pallas kernels for 0%

profile of v1, /device:TPU:4, one launch (start us, length us, event | category | flops | bytes accessed | tf_op | source)
XLA Modules:
  0.0 238.3 jit_solution(6322683524384532719)
XLA Ops:
  7.2 2.1 copy.72
  9.3 5.6 %all-to-all-start = ((bf16[128,8,256]{0,2,1:T(8,128)(2,1)}), bf16[128,8,256]{0,2,1:T(8,128)(2,1)S(1)}, u32[]{:S(2)}, u32[]{:S(2)}) async-start(bf16[128,8,256]{0,2,1:T(8,128)(2,1)} %bitcast.3), calls=%async_computation | async-start | bytes 1048576 | tf_op jit(solution)/shard_map/all_to_all | solution.py:109
  14.9 2.0 copy.74
  17.0 5.1 %all-to-all-done = bf16[128,8,256]{0,2,1:T(8,128)(2,1)S(1)} async-done(((bf16[128,8,256]{0,2,1:T(8,128)(2,1)}), bf16[128,8,256]{0,2,1:T(8,128)(2,1)S(1)}, u32[]{:S(2)}, u32[]{:S(2)}) %all-to-all-start) | async-done | bytes 524320 | tf_op jit(solution)/shard_map/all_to_all | solution.py:109
  22.1 6.6 %all-to-all-start.1 = ((bf16[128,8,256]{0,2,1:T(8,128)(2,1)}), bf16[128,8,256]{0,2,1:T(8,128)(2,1)S(1)}, u32[]{:S(2)}, u32[]{:S(2)}) async-start(bf16[128,8,256]{0,2,1:T(8,128)(2,1)} %bitcast.6), calls=%async_computation.1 | async-start | bytes 1048576 | tf_op jit(solution)/shard_map/all_to_all | solution.py:110
  28.7 1.0 copy.76
  29.7 6.2 %all-to-all-done.1 = bf16[128,8,256]{0,2,1:T(8,128)(2,1)S(1)} async-done(((bf16[128,8,256]{0,2,1:T(8,128)(2,1)}), bf16[128,8,256]{0,2,1:T(8,128)(2,1)S(1)}, u32[]{:S(2)}, u32[]{:S(2)}) %all-to-all-start.1) | async-done | bytes 524320 | tf_op jit(solution)/shard_map/all_to_all | solution.py:110
  35.8 6.6 %all-to-all-start.2 = ((bf16[128,8,256]{0,2,1:T(8,128)(2,1)}), bf16[128,8,256]{0,2,1:T(8,128)(2,1)S(1)}, u32[]{:S(2)}, u32[]{:S(2)}) async-start(bf16[128,8,256]{0,2,1:T(8,128)(2,1)} %bitcast.9), calls=%async_computation.2 | async-start | bytes 1048576 | tf_op jit(solution)/shard_map/all_to_all | solution.py:111
  43.2 6.3 %all-to-all-done.2 = bf16[128,8,256]{0,2,1:T(8,128)(2,1)S(1)} async-done(((bf16[128,8,256]{0,2,1:T(8,128)(2,1)}), bf16[128,8,256]{0,2,1:T(8,128)(2,1)S(1)}, u32[]{:S(2)}, u32[]{:S(2)}) %all-to-all-start.2) | async-done | bytes 524320 | tf_op jit(solution)/shard_map/all_to_all | solution.py:111
  50.9 2.5 %fusion.1 = (f32[1024]{0:T(1024)S(1)}, f32[1024]{0:T(1024)S(1)}, pred[1024,1024]{0,1:T(32,128)(4,1)S(1)}, f32[1024,1024]{0,1:T(8,128)S(1)}) fusion(f32[1024,1024]{0,1:T(8,128)S(1)} %fusion.21, s32[1024]{0:T(1024)S(1)} %add_select_fusion, pred[128,8,8,128]{3,2,1,0:T(8,128)(4,1)S(1)} %bitcast.97, s32[1024]{0:T(1024)S(1)} %convert_reduce_fusion, ...), kind=kOutput, calls=%fused_computation.8 | convolution fusion | flops 278919168 | bytes 11034624 | tf_op jit(solution)/shard_map/dot_general | solution.py:55
  53.4 2.2 fusion.5
  55.6 1.5 convolution_convert_fusion.4
  57.2 1.5 convolution_convert_fusion.3
  58.8 0.9 copy_bitcast_fusion.3
  59.6 6.6 %all-to-all-start.3 = ((bf16[8,128,256]{1,2,0:T(8,128)(2,1)}), bf16[8,128,256]{1,2,0:T(8,128)(2,1)S(1)}, u32[]{:S(2)}, u32[]{:S(2)}) async-start(bf16[8,128,256]{1,2,0:T(8,128)(2,1)} %copy_bitcast_fusion.3), calls=%async_computation.3 | async-start | bytes 1048576 | tf_op jit(solution)/shard_map/all_to_all | solution.py:128
  66.3 7.1 %all-to-all-done.3 = bf16[8,128,256]{1,2,0:T(8,128)(2,1)S(1)} async-done(((bf16[8,128,256]{1,2,0:T(8,128)(2,1)}), bf16[8,128,256]{1,2,0:T(8,128)(2,1)S(1)}, u32[]{:S(2)}, u32[]{:S(2)}) %all-to-all-start.3) | async-done | bytes 524320 | tf_op jit(solution)/shard_map/all_to_all | solution.py:128
  73.4 3.9 %multiply_reduce_fusion = (f32[128]{0:T(128)S(1)}, f32[128,1536]{1,0:T(8,128)S(1)}) fusion(bf16[128,1536]{1,0:T(8,128)(2,1)} %param.12, bf16[128,2048]{0,1:T(8,128)(2,1)S(1)} %bitcast.86, bf16[2048,1536]{1,0:T(8,128)(2,1)} %param.13), kind=kOutput, calls=%fused_computation.36 | convolution fusion | flops 806092672 | bytes 7995904 | tf_op jit(solution)/shard_map/dot_general | solution.py:129
  77.4 8.4 %all_to_all.150 = f32[8,1,4]{2,1,0:T(1,128)S(1)} all-to-all(f32[8,1,4]{2,1,0:T(1,128)S(1)} %broadcast_in_dim.22), channel_id=1, replica_groups=mesh['dp_0'=8,'dp_1'=4,'ctx'=8] {'ctx'}, dimensions={0} | all-to-all | bytes 256 | tf_op jit(solution)/shard_map/all_to_all | solution.py:19
  86.5 1.3 broadcast_in_dim.23
  87.8 10.8 %all-to-all-start.5 = ((f32[32,1,1]{2,1,0:T(1,128)}), f32[32,1,1]{2,1,0:T(1,128)S(1)}, u32[]{:S(2)}, u32[]{:S(2)}) async-start(f32[32,1,1]{2,1,0:T(1,128)} %broadcast_in_dim.23), calls=%async_computation.5 | async-start | bytes 32768 | tf_op jit(solution)/shard_map/all_to_all | solution.py:19
  99.3 8.9 %all-to-all-done.5 = f32[32,1,1]{2,1,0:T(1,128)S(1)} async-done(((f32[32,1,1]{2,1,0:T(1,128)}), f32[32,1,1]{2,1,0:T(1,128)S(1)}, u32[]{:S(2)}, u32[]{:S(2)}) %all-to-all-start.5) | async-done | bytes 160 | tf_op jit(solution)/shard_map/all_to_all | solution.py:19
  109.7 2.0 stack.2
  111.8 6.8 %all-to-all-start.6 = ((bf16[8,128,1536]{2,1,0:T(8,128)(2,1)}), bf16[8,128,1536]{2,1,0:T(8,128)(2,1)}, u32[]{:S(2)}, u32[]{:S(2)}) async-start(bf16[8,128,1536]{2,1,0:T(8,128)(2,1)} %stack.2), calls=%async_computation.6 | async-start | bytes 6291456 | tf_op jit(solution)/shard_map/all_to_all | solution.py:151
  118.5 35.4 %all-to-all-done.6 = bf16[8,128,1536]{2,1,0:T(8,128)(2,1)} async-done(((bf16[8,128,1536]{2,1,0:T(8,128)(2,1)}), bf16[8,128,1536]{2,1,0:T(8,128)(2,1)}, u32[]{:S(2)}, u32[]{:S(2)}) %all-to-all-start.6) | async-done | bytes 3145760 | tf_op jit(solution)/shard_map/all_to_all | solution.py:151
  153.9 4.1 %fusion.3 = bf16[256,1536]{0,1:T(8,128)(2,1)} fusion(bf16[1024,1536]{1,0:T(8,128)(2,1)} %bitcast.19, bf16[1024,128]{0,1:T(8,128)(2,1)S(1)} %convolution_convert_fusion.3, bf16[1024,128]{0,1:T(8,128)(2,1)S(1)} %convolution_convert_fusion.4), kind=kOutput, calls=%fused_computation.11 | convolution fusion | flops 807141376 | bytes 4456448 | tf_op jit(solution)/shard_map/dot_general | solution.py:158
  158.0 3.2 %convolution_convert_fusion = bf16[1024,256]{0,1:T(8,128)(2,1)S(1)} fusion(bf16[1024,1536]{1,0:T(8,128)(2,1)} %bitcast.19, bf16[2048,1536]{1,0:T(8,128)(2,1)} %param.13, s32[]{:T(128)S(6)} %select_n.38), kind=kOutput, calls=%fused_computation.17 | convolution fusion | flops 805568512 | bytes 4456452 | tf_op jit(solution)/shard_map/dot_general | solution.py:154
  161.4 1.6 convolution_convert_fusion.2
  163.6 2.3 convolution_convert_fusion.1
  166.0 5.0 %multiply_convert_fusion.1 = bf16[1024,1024]{0,1:T(8,128)(2,1)S(1)} fusion(f32[1024]{0:T(1024)S(1)} %get-tuple-element.20, bf16[1024,256]{1,0:T(8,128)(2,1)S(1)} %bitcast.100, bf16[1024,256]{0,1:T(8,128)(2,1)} %copy-done.13, f32[1024]{0:T(1024)S(1)} %get-tuple-element.16, pred[1024,1024]{0,1:T(32,128)(4,1)} %copy-done.8, f32[1024]{0:T(1024)S(1)} %get-tuple-element.18, ...), kind=kOutput, calls=%fused_computation.1 | convolution fusion | flops 276824064 | bytes 7876608 | tf_op jit(solution)/shard_map/dot_general | solution.py:74
  171.0 3.1 %multiply_convert_fusion = bf16[1024,1024]{0,1:T(8,128)(2,1)} fusion(f32[1024]{0:T(1024)S(1)} %get-tuple-element.21, bf16[1024,256]{1,0:T(8,128)(2,1)S(1)} %bitcast.101, bf16[1024,256]{0,1:T(8,128)(2,1)S(1)} %copy-done.14, f32[1024]{0:T(1024)S(1)} %get-tuple-element.17, pred[1024,1024]{0,1:T(32,128)(4,1)S(1)} %copy-done.9, f32[1024]{0:T(1024)S(1)} %get-tuple-element.19, ...), kind=kOutput, calls=%fused_computation | convolution fusion | flops 276824064 | bytes 7876608 | tf_op jit(solution)/shard_map/dot_general | solution.py:74
  174.1 0.9 copy_bitcast_fusion
  175.0 6.6 %all-to-all-start.9 = ((bf16[8,128,256]{1,2,0:T(8,128)(2,1)}), bf16[8,128,256]{1,2,0:T(8,128)(2,1)S(1)}, u32[]{:S(2)}, u32[]{:S(2)}) async-start(bf16[8,128,256]{1,2,0:T(8,128)(2,1)} %copy_bitcast_fusion), calls=%async_computation.9 | async-start | bytes 1048576 | tf_op jit(solution)/shard_map/all_to_all | solution.py:185
  181.6 0.8 fusion.10
  182.4 2.4 %fusion.11 = bf16[1024,128]{0,1:T(8,128)(2,1)S(1)} fusion(bf16[1024,1024]{0,1:T(8,128)(2,1)} %multiply_convert_fusion, bf16[1024,256]{1,0:T(8,128)(2,1)S(1)} %bitcast.85), kind=kOutput, calls=%fused_computation.29 | convolution fusion | flops 268697600 | bytes 2621440 | tf_op jit(solution)/shard_map/dot_general | solution.py:83
  184.8 0.9 copy_bitcast_fusion.1
  185.7 3.0 %all-to-all-done.9 = bf16[8,128,256]{1,2,0:T(8,128)(2,1)S(1)} async-done(((bf16[8,128,256]{1,2,0:T(8,128)(2,1)}), bf16[8,128,256]{1,2,0:T(8,128)(2,1)S(1)}, u32[]{:S(2)}, u32[]{:S(2)}) %all-to-all-start.9) | async-done | bytes 524320 | tf_op jit(solution)/shard_map/all_to_all | solution.py:185
  188.7 6.6 %all-to-all-start.8 = ((bf16[8,128,256]{1,2,0:T(8,128)(2,1)}), bf16[8,128,256]{1,2,0:T(8,128)(2,1)S(1)}, u32[]{:S(2)}, u32[]{:S(2)}) async-start(bf16[8,128,256]{1,2,0:T(8,128)(2,1)} %copy_bitcast_fusion.1), calls=%async_computation.8 | async-start | bytes 1048576 | tf_op jit(solution)/shard_map/all_to_all | solution.py:182
  195.3 1.6 fusion.8
  197.6 0.9 copy_bitcast_fusion.2
  198.5 4.0 %all-to-all-done.8 = bf16[8,128,256]{1,2,0:T(8,128)(2,1)S(1)} async-done(((bf16[8,128,256]{1,2,0:T(8,128)(2,1)}), bf16[8,128,256]{1,2,0:T(8,128)(2,1)S(1)}, u32[]{:S(2)}, u32[]{:S(2)}) %all-to-all-start.8) | async-done | bytes 524320 | tf_op jit(solution)/shard_map/all_to_all | solution.py:182
  202.5 6.6 %all-to-all-start.7 = ((bf16[8,128,256]{1,2,0:T(8,128)(2,1)}), bf16[8,128,256]{1,2,0:T(8,128)(2,1)S(1)}, u32[]{:S(2)}, u32[]{:S(2)}) async-start(bf16[8,128,256]{1,2,0:T(8,128)(2,1)} %copy_bitcast_fusion.2), calls=%async_computation.7 | async-start | bytes 1048576 | tf_op jit(solution)/shard_map/all_to_all | solution.py:179
  209.1 0.7 reduce-scatter.5.cloned.1.call-update
  209.8 1.0 copy.88
  210.8 1.0 copy.87
  211.8 4.4 %all-to-all-done.7 = bf16[8,128,256]{1,2,0:T(8,128)(2,1)S(1)} async-done(((bf16[8,128,256]{1,2,0:T(8,128)(2,1)}), bf16[8,128,256]{1,2,0:T(8,128)(2,1)S(1)}, u32[]{:S(2)}, u32[]{:S(2)}) %all-to-all-start.7) | async-done | bytes 524320 | tf_op jit(solution)/shard_map/all_to_all | solution.py:179
  216.2 1.0 copy.86
  217.2 12.8 %reduce-scatter.5.cloned.1.call-done = bf16[256,48]{0,1:T(8,128)(2,1)} async-done(((bf16[256,192]{0,1:T(8,128)(2,1)}), bf16[256,48]{0,1:T(8,128)(2,1)}) %reduce-scatter.5.cloned.1.call-update) | async-done | bytes 24592 | tf_op jit(solution)/shard_map/reduce_scatter | solution.py:30
  230.1 1.4 convert_element_type.106
  (64 shorter events, 5.3 us)
Async XLA Ops:
  7.2 21.5 %copy-start.10 = (bf16[128,2048]{1,0:T(8,128)(2,1)S(1)}, bf16[128,2048]{1,0:T(8,128)(2,1)}, u32[]{:S(2)}) copy-start(bf16[128,2048]{1,0:T(8,128)(2,1)} %param.11) | copy-start | bytes 1572868
  7.2 35.2 %copy-start.16 = (s32[1,8,8]{2,1,0:T(8,128)S(1)}, s32[1,8,8]{2,1,0:T(8,128)}, u32[]{:S(2)}) copy-start(s32[1,8,8]{2,1,0:T(8,128)} %param.16) | copy-start | bytes 772
  7.2 35.3 %copy-start.17 = (s32[1,4]{1,0:T(1,128)S(1)}, s32[1,4]{1,0:T(1,128)}, u32[]{:S(2)}) copy-start(s32[1,4]{1,0:T(1,128)} %param.14) | copy-start | bytes 52
  9.3 12.8 %all-to-all-start = ((bf16[128,8,256]{0,2,1:T(8,128)(2,1)}), bf16[128,8,256]{0,2,1:T(8,128)(2,1)S(1)}, u32[]{:S(2)}, u32[]{:S(2)}) async-start(bf16[128,8,256]{0,2,1:T(8,128)(2,1)} %bitcast.3), calls=%async_computation | async-start | bytes 1048576 | tf_op jit(solution)/shard_map/all_to_all | solution.py:109
  22.1 13.7 %all-to-all-start.1 = ((bf16[128,8,256]{0,2,1:T(8,128)(2,1)}), bf16[128,8,256]{0,2,1:T(8,128)(2,1)S(1)}, u32[]{:S(2)}, u32[]{:S(2)}) async-start(bf16[128,8,256]{0,2,1:T(8,128)(2,1)} %bitcast.6), calls=%async_computation.1 | async-start | bytes 1048576 | tf_op jit(solution)/shard_map/all_to_all | solution.py:110
  35.8 13.7 %all-to-all-start.2 = ((bf16[128,8,256]{0,2,1:T(8,128)(2,1)}), bf16[128,8,256]{0,2,1:T(8,128)(2,1)S(1)}, u32[]{:S(2)}, u32[]{:S(2)}) async-start(bf16[128,8,256]{0,2,1:T(8,128)(2,1)} %bitcast.9), calls=%async_computation.2 | async-start | bytes 1048576 | tf_op jit(solution)/shard_map/all_to_all | solution.py:111
  43.2 10.1 %copy-start.6 = (bf16[8,128,256]{2,1,0:T(8,128)(2,1)}, bf16[8,128,256]{2,1,0:T(8,128)(2,1)S(1)}, u32[]{:S(2)}) copy-start(bf16[8,128,256]{2,1,0:T(8,128)(2,1)S(1)} %copy.75) | copy-start | bytes 1572868
  49.8 7.4 %copy-start.11 = (bf16[8,128,256]{2,1,0:T(8,128)(2,1)}, bf16[8,128,256]{2,1,0:T(8,128)(2,1)S(1)}, u32[]{:S(2)}) copy-start(bf16[8,128,256]{2,1,0:T(8,128)(2,1)S(1)} %copy.77) | copy-start | bytes 1572868
  50.5 6.7 %copy-start = (f32[1024,1024]{0,1:T(8,128)}, f32[1024,1024]{0,1:T(8,128)S(1)}, u32[]{:S(2)}) copy-start(f32[1024,1024]{0,1:T(8,128)S(1)} %fusion.21) | copy-start | bytes 12582916
  53.4 2.3 copy-start.3
  53.4 109.6 %copy-start.8 = (pred[1024,1024]{0,1:T(32,128)(4,1)}, pred[1024,1024]{0,1:T(32,128)(4,1)S(1)}, u32[]{:S(2)}) copy-start(pred[1024,1024]{0,1:T(32,128)(4,1)S(1)} %get-tuple-element.22) | copy-start | bytes 3145732
  59.6 13.7 %all-to-all-start.3 = ((bf16[8,128,256]{1,2,0:T(8,128)(2,1)}), bf16[8,128,256]{1,2,0:T(8,128)(2,1)S(1)}, u32[]{:S(2)}, u32[]{:S(2)}) async-start(bf16[8,128,256]{1,2,0:T(8,128)(2,1)} %copy_bitcast_fusion.3), calls=%async_computation.3 | async-start | bytes 1048576 | tf_op jit(solution)/shard_map/all_to_all | solution.py:128
  66.2 19.7 %copy-start.18 = (s32[1,4]{1,0:T(1,128)S(1)}, s32[1,4]{1,0:T(1,128)}, u32[]{:S(2)}) copy-start(s32[1,4]{1,0:T(1,128)} %param.15) | copy-start | bytes 52
  87.8 20.4 %all-to-all-start.5 = ((f32[32,1,1]{2,1,0:T(1,128)}), f32[32,1,1]{2,1,0:T(1,128)S(1)}, u32[]{:S(2)}, u32[]{:S(2)}) async-start(f32[32,1,1]{2,1,0:T(1,128)} %broadcast_in_dim.23), calls=%async_computation.5 | async-start | bytes 32768 | tf_op jit(solution)/shard_map/all_to_all | solution.py:19
  111.8 42.1 %all-to-all-start.6 = ((bf16[8,128,1536]{2,1,0:T(8,128)(2,1)}), bf16[8,128,1536]{2,1,0:T(8,128)(2,1)}, u32[]{:S(2)}, u32[]{:S(2)}) async-start(bf16[8,128,1536]{2,1,0:T(8,128)(2,1)} %stack.2), calls=%async_computation.6 | async-start | bytes 6291456 | tf_op jit(solution)/shard_map/all_to_all | solution.py:151
  118.5 90.6 %reduce-scatter.3.cloned.1.call-start = ((), (), s32[]{:S(2)}) async-start(), calls=%async_computation.12 | async-start | bytes 884736 | tf_op jit(solution)/shard_map/reduce_scatter | solution.py:30
  158.0 3.4 %copy-start.4 = (f32[1024,1024]{0,1:T(8,128)S(1)}, f32[1024,1024]{0,1:T(8,128)}, u32[]{:S(2)}) copy-start(f32[1024,1024]{0,1:T(8,128)} %copy-done.3) | copy-start | bytes 12582916
  161.2 1.8 copy-start.13
  161.4 2.2 copy-start.1
  163.6 2.3 copy-start.12
  165.9 5.1 %copy-start.2 = (f32[1024,1024]{0,1:T(8,128)S(1)}, f32[1024,1024]{0,1:T(8,128)}, u32[]{:S(2)}) copy-start(f32[1024,1024]{0,1:T(8,128)} %copy-done) | copy-start | bytes 12582916
  165.9 5.1 %copy-start.9 = (pred[1024,1024]{0,1:T(32,128)(4,1)S(1)}, pred[1024,1024]{0,1:T(32,128)(4,1)}, u32[]{:S(2)}) copy-start(pred[1024,1024]{0,1:T(32,128)(4,1)} %copy-done.8) | copy-start | bytes 3145732
  165.9 5.1 %copy-start.14 = (bf16[1024,256]{0,1:T(8,128)(2,1)S(1)}, bf16[1024,256]{0,1:T(8,128)(2,1)}, u32[]{:S(2)}) copy-start(bf16[1024,256]{0,1:T(8,128)(2,1)} %copy-done.13) | copy-start | bytes 1572868
  171.0 3.1 %copy-start.15 = (bf16[1024,128]{0,1:T(8,128)(2,1)S(1)}, bf16[1024,128]{0,1:T(8,128)(2,1)}, u32[]{:S(2)}) copy-start(bf16[1024,128]{0,1:T(8,128)(2,1)} %convolution_convert_fusion.1) | copy-start | bytes 786436
  175.0 13.7 %all-to-all-start.9 = ((bf16[8,128,256]{1,2,0:T(8,128)(2,1)}), bf16[8,128,256]{1,2,0:T(8,128)(2,1)S(1)}, u32[]{:S(2)}, u32[]{:S(2)}) async-start(bf16[8,128,256]{1,2,0:T(8,128)(2,1)} %copy_bitcast_fusion), calls=%async_computation.9 | async-start | bytes 1048576 | tf_op jit(solution)/shard_map/all_to_all | solution.py:185
  188.7 13.7 %all-to-all-start.8 = ((bf16[8,128,256]{1,2,0:T(8,128)(2,1)}), bf16[8,128,256]{1,2,0:T(8,128)(2,1)S(1)}, u32[]{:S(2)}, u32[]{:S(2)}) async-start(bf16[8,128,256]{1,2,0:T(8,128)(2,1)} %copy_bitcast_fusion.1), calls=%async_computation.8 | async-start | bytes 1048576 | tf_op jit(solution)/shard_map/all_to_all | solution.py:182
  195.3 1.7 copy-start.5
  195.3 1.8 copy-start.7
  202.5 13.7 %all-to-all-start.7 = ((bf16[8,128,256]{1,2,0:T(8,128)(2,1)}), bf16[8,128,256]{1,2,0:T(8,128)(2,1)S(1)}, u32[]{:S(2)}, u32[]{:S(2)}) async-start(bf16[8,128,256]{1,2,0:T(8,128)(2,1)} %copy_bitcast_fusion.2), calls=%async_computation.7 | async-start | bytes 1048576 | tf_op jit(solution)/shard_map/all_to_all | solution.py:179
  209.1 21.0 %reduce-scatter.5.cloned.1.call-start = ((), (), s32[]{:S(2)}) async-start(), calls=%async_computation.13 | async-start | bytes 122880 | tf_op jit(solution)/shard_map/reduce_scatter | solution.py:30
Sparse Core Ops, SparseCore 0:
  166.0 33.5 reduce-scatter.2
  212.4 17.6 reduce-scatter.4
